TPU v7x, 128 devices: a whole 4x4x4 slice. The times are simulated.
128 devices in a mesh: req: 32 (over z_lo, y, x), tp: 4 (over z_hi, core).
Axes of the slice: x: 4, y: 4, z: 4 (z_hi: 2, z_lo: 2; z = z_hi * 2 + z_lo), core: 2. Of those that a mesh axis runs over, the one named last changes fastest.
Arguments:
- hidden_in: bfloat16 [8192, 2304], P('req'), may hold values from -6 to 6
- cache_lengths: int32 [32], P('req'), may hold values from 128 to 2048, as said below
- key_cache: bfloat16 [32, 2048, 2304], P('req', None, 'tp'), may hold values from -104 to 104
- value_cache: bfloat16 [32, 2048, 2304], P('req', None, 'tp'), may hold values from -6 to 6
- attn_norm: float32 [2304], replicated, may hold values from 0.5 to 1.5
- w_qkv: bfloat16 [3, 2304, 2304], P(None, None, 'tp'), may hold values from -0.125 to 0.125
- w_out: bfloat16 [2304, 2304], P('tp'), may hold values from -0.125 to 0.125
- ffn_norm: float32 [2304], replicated, may hold values from 0.5 to 1.5
- router: bfloat16 [2304, 8], replicated, may hold values from -0.125 to 0.125
- routes: int32 [8192, 2], P('req'), may hold values from 0 to 7, all different within a row; in each aligned block of 256 rows (0 to 255, 256 to 511, ...) at most 96 rows name the same one
- expert_gate: bfloat16 [32, 2304, 1440], P('req', None, 'tp'), may hold values from -0.125 to 0.125
- expert_up: bfloat16 [32, 2304, 1440], P('req', None, 'tp'), may hold values from -0.125 to 0.125
- expert_down: bfloat16 [32, 1440, 2304], P('req', 'tp'), may hold values from -0.078125 to 0.078125
Outputs:
- block_out: bfloat16 [8192, 2304], P(('req', 'tp'))
Inputs may be any that keep to these rules, and one draw needn't show every extreme that they name: `cache_lengths`: some request has exactly 2048 cached tokens. `routes`: within the 256 rows of one request no expert is named by more than 96 rows, and in every draw, within some request, an expert is named by exactly 96 rows; a row's two experts differ.
All inputs are finite; a program needn't handle non-finite values.
Results may differ from a plain program's by a relative error of at most 0.013.
Values may be sent and summed in bfloat16 or wider, within the bound.
A program may use at most 192 MiB of HBM per device.

v0:
```python
import math

import jax
import jax.numpy as jnp
from jax import lax
from jax.sharding import PartitionSpec as P

HEAD = 64
TOP = 2
CAP = 96


EPSILON = 1e-05


def normalize(inputs, scale_gain):
    mean_square = jnp.mean(inputs * inputs, axis=-1, keepdims=True)
    return inputs * lax.rsqrt(mean_square + EPSILON) * scale_gain


def rotate(inputs, positions):
    half_dim = inputs.shape[-1] // 2
    frequency = jnp.exp(
        jnp.arange(half_dim, dtype=jnp.float32) * (-2.0 * math.log(10000.0) / inputs.shape[-1])
    )
    angles = positions.astype(jnp.float32)[:, None] * frequency[None, :]
    cosine = jnp.cos(angles)[:, None, :]
    sine_part = jnp.sin(angles)[:, None, :]
    lower_half = inputs[..., :half_dim]
    upper_half = inputs[..., half_dim:]
    return jnp.concatenate(
        [
            lower_half * cosine - upper_half * sine_part,
            lower_half * sine_part + upper_half * cosine,
        ],
        axis=-1,
    )


def attention(queries, all_keys, all_values, length):
    query_count = queries.shape[0]
    cache_len = all_keys.shape[0] - query_count
    scores = jnp.einsum(
        "qhd,khd->hqk", queries, all_keys, preferred_element_type=jnp.float32
    ) * queries.shape[-1] ** (-0.5)
    slot_ids = jnp.arange(cache_len + query_count, dtype=jnp.int32)
    query_ids = jnp.arange(query_count, dtype=jnp.int32)
    is_live = jnp.where(
        slot_ids[None, :] < cache_len,
        slot_ids[None, :] < length,
        slot_ids[None, :] - cache_len <= query_ids[:, None],
    )
    scores = jnp.where(is_live[None], scores, -jnp.inf)
    row_max = jnp.max(scores, axis=-1, keepdims=True)
    weights = jnp.exp(scores - row_max)
    totals = jnp.sum(weights, axis=-1)
    mixture = jnp.einsum(
        "hqk,khd->qhd", weights.astype(jnp.bfloat16), all_values, preferred_element_type=jnp.float32
    )
    return (mixture / jnp.transpose(totals)[:, :, None]).astype(jnp.bfloat16)


def per_device(
    hidden_in,
    cache_lengths,
    key_cache,
    value_cache,
    attn_norm,
    w_qkv,
    w_out,
    ffn_norm,
    router,
    routes,
    expert_gate,
    expert_up,
    expert_down,
):
    token_count = hidden_in.shape[0]
    model_width = hidden_in.shape[1]
    local_lanes = w_qkv.shape[2]
    local_heads = local_lanes // HEAD
    cache_len = key_cache.shape[1]
    token_share = token_count // lax.axis_size("tp")
    offset = lax.axis_index("tp") * token_share
    expert_count = router.shape[1]
    copies = lax.axis_size("req") // expert_count
    residual = hidden_in.astype(jnp.float32)
    normed = normalize(residual, attn_norm).astype(jnp.bfloat16)
    projected = jnp.einsum("td,cdh->cth", normed, w_qkv, preferred_element_type=jnp.float32)
    length = cache_lengths[0]
    positions = length + jnp.arange(token_count, dtype=jnp.int32)
    queries = rotate(projected[0].reshape(token_count, local_heads, HEAD), positions).astype(
        jnp.bfloat16
    )
    fresh_keys = rotate(projected[1].reshape(token_count, local_heads, HEAD), positions).astype(
        jnp.bfloat16
    )
    fresh_values = projected[2].reshape(token_count, local_heads, HEAD).astype(jnp.bfloat16)
    all_keys = jnp.concatenate(
        [key_cache[0].reshape(cache_len, local_heads, HEAD), fresh_keys], axis=0
    )
    all_values = jnp.concatenate(
        [value_cache[0].reshape(cache_len, local_heads, HEAD), fresh_values], axis=0
    )
    attended = attention(queries, all_keys, all_values, length).reshape(token_count, local_lanes)
    summed_attn = lax.psum(
        jnp.dot(attended, w_out, preferred_element_type=jnp.float32).astype(jnp.bfloat16), "tp"
    ).astype(jnp.float32)
    updated = residual + summed_attn
    moe_input = normalize(updated, ffn_norm).astype(jnp.bfloat16)
    own_residual = lax.dynamic_slice_in_dim(updated, offset, token_share, 0)
    logits = jnp.dot(moe_input, router, preferred_element_type=jnp.float32)
    chosen = jnp.take_along_axis(logits, routes, axis=1)
    first_gate = 1.0 / (1.0 + jnp.exp(chosen[:, 1] - chosen[:, 0]))
    second_gate = 1.0 / (1.0 + jnp.exp(chosen[:, 0] - chosen[:, 1]))
    flat_routes = routes.reshape(-1)
    onehot = (flat_routes[:, None] == jnp.arange(expert_count, dtype=jnp.int32)[None, :]).astype(
        jnp.int32
    )
    slot_rank = jnp.sum((jnp.cumsum(onehot, axis=0) - onehot) * onehot, axis=1)
    slot_ids = flat_routes * CAP + slot_rank
    paired = slot_ids.reshape(token_count, TOP)
    placing = jnp.any(
        paired[None, :, :] == jnp.arange(expert_count * CAP, dtype=jnp.int32)[:, None, None], axis=2
    ).astype(jnp.bfloat16)
    packed = (
        jnp.dot(placing, moe_input, preferred_element_type=jnp.float32)
        .astype(jnp.bfloat16)
        .reshape(expert_count, CAP, model_width)
    )
    outgoing = jnp.broadcast_to(packed[:, None], (expert_count, copies, CAP, model_width)).reshape(
        expert_count * copies, CAP, model_width
    )
    received = lax.all_to_all(outgoing, "req", split_axis=0, concat_axis=0, tiled=True)
    token_rows = received.reshape(-1, model_width)
    gate_proj = jnp.dot(token_rows, expert_gate[0], preferred_element_type=jnp.float32)
    up_proj = jnp.dot(token_rows, expert_up[0], preferred_element_type=jnp.float32)
    activation = (jax.nn.silu(gate_proj) * up_proj).astype(jnp.bfloat16)
    partial_value = jnp.dot(activation, expert_down[0], preferred_element_type=jnp.float32).astype(
        jnp.bfloat16
    )
    returned = lax.all_to_all(
        partial_value.reshape(received.shape), "req", split_axis=0, concat_axis=0, tiled=True
    )
    back_rows = returned.reshape(-1, model_width)
    back_index = (
        flat_routes[None, :] * copies + jnp.arange(copies, dtype=jnp.int32)[:, None]
    ) * CAP + slot_rank[None, :]
    fetched = jnp.take(back_rows, back_index, axis=0)
    summed = jnp.sum(fetched.astype(jnp.float32), axis=0).reshape(token_count, TOP, model_width)
    local_sum = first_gate[:, None] * summed[:, 0] + second_gate[:, None] * summed[:, 1]
    moe_own = lax.psum_scatter(
        local_sum.astype(jnp.bfloat16), "tp", scatter_dimension=0, tiled=True
    ).astype(jnp.float32)
    return (own_residual + moe_own).astype(jnp.bfloat16)


def solution(mesh):
    return jax.shard_map(
        per_device,
        mesh=mesh,
        in_specs=(
            P("req", None),
            P("req"),
            P("req", None, "tp"),
            P("req", None, "tp"),
            P(),
            P(None, None, "tp"),
            P("tp", None),
            P(),
            P(),
            P("req", None),
            P("req", None, "tp"),
            P("req", None, "tp"),
            P("req", "tp", None),
        ),
        out_specs=P(("req", "tp"), None),
        check_vma=False,
    )
```

profile of v0, /device:TPU:1, one launch (start us, length us, event | category | flops | bytes accessed | tf_op | source)
XLA Modules:
  0.0 635.5 jit_solution(16440981270016864668)
XLA Ops:
  6.5 0.0 copy-start
  6.5 0.0 all-reduce.2.cloned.1.call-start
  6.6 1.7 fusion.16
  8.3 6.0 convolution_bitcast_fusion
  14.3 0.0 copy-start.7
  14.4 0.1 fusion.64
  15.3 0.2 multiply_cosine_fusion
  15.5 0.4 fusion.23
  15.9 0.2 subtract_convert_fusion.1
  16.1 0.0 copy-done.7
  16.1 9.9 %fusion = (f32[9,256]{1,0:T(8,128)S(1)}, f32[9,256,2304]{2,1,0:T(8,128)}) fusion(pred[256,2304]{1,0:T(8,128)(4,1)S(1)} %fusion.23, bf16[256,9,32]{0,2,1:T(8,128)(2,1)S(1)} %get-tuple-element.15, bf16[256,9,32]{0,2,1:T(8,128)(2,1)S(1)} %get-tuple-element.16, bf16[2048,9,64]{0,2,1:T(8,128)(2,1)S(1)} %bitcast.90, ...), kind=kOutput, calls=%fused_computation.5 | convolution fusion | flops 703952640 | bytes 24781824 | tf_op jit(solution)/shard_map/qhd,khd->hqk/dot_general | solution.py:43
  26.0 0.0 copy-start.8
  26.0 10.6 %fusion.1 = f32[9,256]{1,0:T(8,128)S(1)} fusion(f32[9,256,2304]{2,1,0:T(8,128)} %get-tuple-element.22, f32[9,256]{1,0:T(8,128)S(1)} %get-tuple-element.21, pred[256,2304]{1,0:T(8,128)(4,1)S(1)} %fusion.23), kind=kLoop, calls=%fused_computation.7 | loop fusion | flops 21231360 | bytes 21841920 | tf_op jit(solution)/shard_map/reduce_sum | solution.py:56
  36.6 0.0 copy-done.8
  36.6 10.0 %fusion.45 = bf16[256,9,64]{0,2,1:T(8,128)(2,1)S(1)} fusion(f32[9,256,2304]{2,1,0:T(8,128)} %get-tuple-element.22, f32[9,256]{1,0:T(8,128)S(1)} %get-tuple-element.21, pred[256,2304]{1,0:T(8,128)(4,1)S(1)} %fusion.23, bf16[256,9,64]{0,2,1:T(8,128)(2,1)S(1)} %bitcast.85, bf16[2048,9,64]{0,2,1:T(8,128)(2,1)S(1)} %bitcast.91, f32[256,9]{0,1:T(8,128)S(1)} %bitcast.87), kind=kOutput, calls=%fused_computation.53 | convolution fusion | flops 706314240 | bytes 24791040 | tf_op jit(solution)/shard_map/hqk,khd->qhd/dot_general | solution.py:57
  46.6 0.0 copy-done
  46.7 0.0 copy-start.5
  46.7 2.2 convolution_convert_fusion.2
  48.8 0.0 all-reduce.2.cloned.1.call-update
  48.9 0.0 copy-done.5
  48.9 0.1 copy.51
  49.0 0.1 broadcast_in_dim_reshape.2
  49.2 0.1 eq.39
  49.3 0.0 copy-start.6
  49.3 1.1 reduce-window.6
  50.5 0.2 slice_reduce_fusion
  50.7 0.1 fusion.54
  50.8 0.1 reduce_sum.51
  51.0 0.1 copy.53
  51.1 0.3 fusion.30
  51.4 47.8 %all-reduce.2.cloned.1.call-done = bf16[256,2304]{1,0:T(8,128)(2,1)} async-done(((bf16[256,2304]{1,0:T(8,128)(2,1)}), bf16[256,2304]{1,0:T(8,128)(2,1)}) %all-reduce.2.cloned.1.call-update) | async-done | bytes 1179664 | tf_op jit(solution)/shard_map/psum | solution.py:106
  99.2 0.0 copy-done.3
  99.2 0.0 copy-start.4
  99.2 3.1 convert_add_fusion
  102.3 0.0 copy-done.6
  102.3 0.0 copy-done.4
  102.3 1.3 convolution_convert_fusion.1
  103.6 1.4 broadcast_in_dim.50
  105.1 0.0 copy-start.9
  105.1 163.3 %all_to_all.10 = bf16[32,96,2304]{2,1,0:T(8,128)(2,1)S(1)} all-to-all(bf16[32,96,2304]{2,1,0:T(8,128)(2,1)S(1)} %bitcast.76), channel_id=1, replica_groups=mesh['req'=32,'tp'=4] {'req'}, dimensions={0} | all-to-all | bytes 28311552 | tf_op jit(solution)/shard_map/all_to_all | solution.py:134
  268.3 5.1 copy-done.2
  273.5 0.0 copy-done.9
  273.5 7.0 %fusion.28 = f32[3072,360]{0,1:T(8,128)} fusion(bf16[3072,2304]{1,0:T(8,128)(2,1)S(1)} %bitcast.80, bf16[1,2304,360]{1,2,0:T(8,128)(2,1)S(1)} %copy-done.9), kind=kOutput, calls=%fused_computation.43 | convolution fusion | flops 5096079360 | bytes 20238336 | tf_op jit(solution)/shard_map/dot_general | solution.py:136
  280.5 20.6 %convolution_convert_fusion = bf16[3072,2304]{1,0:T(8,128)(2,1)} fusion(bf16[3072,2304]{1,0:T(8,128)(2,1)} %bitcast.81, f32[3072,360]{0,1:T(8,128)} %fusion.28, bf16[1,360,2304]{2,1,0:T(8,128)(2,1)} %param.25, bf16[1,2304,360]{1,2,0:T(8,128)(2,1)} %param.24), kind=kOutput, calls=%fused_computation.6 | convolution fusion | flops 10205872128 | bytes 36052992 | tf_op jit(solution)/shard_map/dot_general | solution.py:139
  301.1 5.2 all-to-all-start.1
  306.3 0.0 reduce-scatter.2.cloned.1.call-start
  306.4 0.1 copy.49
  306.5 0.1 reshape.300
  306.7 0.0 copy-done.10
  306.7 0.5 fusion.62
  307.3 3.7 gather_fusion.1
  311.0 0.1 reshape.303
  311.1 0.1 copy.50
  311.2 198.1 %all-to-all-done.1 = bf16[32,96,2304]{2,1,0:T(8,128)(2,1)} async-done(((bf16[32,96,2304]{2,1,0:T(8,128)(2,1)}), bf16[32,96,2304]{2,1,0:T(8,128)(2,1)}, u32[]{:S(2)}, u32[]{:S(2)}) %all-to-all-start.1) | async-done | bytes 14155808 | tf_op jit(solution)/shard_map/all_to_all | solution.py:142
  509.3 25.2 %gather_fusion = bf16[2048,2304]{1,0:T(8,128)(2,1)} fusion(bf16[3072,2304]{1,0:T(8,128)(2,1)} %bitcast.22, s32[2048]{0:T(1024)S(1)} %broadcast_clamp_fusion), kind=kCustom, calls=%fused_computation | custom fusion | bytes 18882560 | tf_op jit(solution)/shard_map/jit(_take)/gather | solution.py:149
  534.5 8.2 %convert_reduce_fusion = f32[512,2304]{1,0:T(8,128)} fusion(bf16[4,512,2304]{2,1,0:T(8,128)(2,1)} %bitcast.77, pred[4,512]{1,0:T(4,128)(4,1)S(1)} %compare_and_fusion), kind=kLoop, calls=%fused_computation.4 | loop fusion | flops 12976128 | bytes 14157824 | tf_op jit(solution)/shard_map/reduce_sum | solution.py:150
  542.7 6.4 %reshape.291 = f32[256,2,2304]{2,1,0:T(2,128)} reshape(f32[512,2304]{1,0:T(8,128)} %convert_reduce_fusion) | data formatting | bytes 9437184 | tf_op jit(solution)/shard_map/reshape | solution.py:150
  549.1 7.8 %fusion.63 = (f32[256,1,2304]{2,1,0:T(1,128)S(1)}, f32[256,1,2304]{2,1,0:T(1,128)S(1)}) fusion(f32[256,2,2304]{2,1,0:T(2,128)} %reshape.291), kind=kLoop, calls=%fused_computation.97 | loop fusion | bytes 9437184 | tf_op jit(solution)/shard_map/slice | solution.py:151
  556.9 0.0 copy-start.1
  556.9 1.4 fusion.21
  558.3 0.0 reduce-scatter.2.cloned.1.call-update
  558.3 68.4 %reduce-scatter.2.cloned.1.call-done = bf16[64,2304]{1,0:T(8,128)(2,1)} async-done(((bf16[256,2304]{1,0:T(8,128)(2,1)}), bf16[64,2304]{1,0:T(8,128)(2,1)}) %reduce-scatter.2.cloned.1.call-update) | async-done | bytes 294928 | tf_op jit(solution)/shard_map/reduce_scatter | solution.py:152
  626.7 1.9 add_convert_fusion
  628.6 0.0 copy-done.1
  (22 shorter events, 0.2 us)
Async XLA Ops:
  6.5 40.1 %copy-start = (bf16[576,2304]{1,0:T(8,128)(2,1)S(1)}, bf16[576,2304]{1,0:T(8,128)(2,1)}, u32[]{:S(2)}) copy-start(bf16[576,2304]{1,0:T(8,128)(2,1)} %param.19) | copy-start | bytes 7962628
  6.5 92.7 %all-reduce.2.cloned.1.call-start = ((), (), s32[]{:S(2)}) async-start(), calls=%async_computation.3 | async-start | bytes 2359296 | tf_op jit(solution)/shard_map/psum | solution.py:106
  14.3 1.7 copy-start.7
  26.0 10.6 %copy-start.8 = (bf16[1,2048,576]{1,2,0:T(8,128)(2,1)S(1)}, bf16[1,2048,576]{1,2,0:T(8,128)(2,1)}, u32[]{:S(2)}) copy-start(bf16[1,2048,576]{1,2,0:T(8,128)(2,1)} %param.16) | copy-start | bytes 7077892
  46.7 2.2 copy-start.5
  48.8 50.4 %copy-start.3 = (bf16[256,2304]{1,0:T(8,128)(2,1)S(1)}, bf16[256,2304]{1,0:T(8,128)(2,1)}, u32[]{:S(2)}) copy-start(bf16[256,2304]{1,0:T(8,128)(2,1)} %param.13) | copy-start | bytes 3538948
  49.3 53.0 %copy-start.6 = (f32[2304]{0:T(1024)S(1)}, f32[2304]{0:T(1024)}, u32[]{:S(2)}) copy-start(f32[2304]{0:T(1024)} %param.20) | copy-start | bytes 27652
  99.2 3.1 copy-start.4
  105.1 168.4 %copy-start.9 = (bf16[1,2304,360]{1,2,0:T(8,128)(2,1)S(1)}, bf16[1,2304,360]{1,2,0:T(8,128)(2,1)}, u32[]{:S(2)}) copy-start(bf16[1,2304,360]{1,2,0:T(8,128)(2,1)} %param.23) | copy-start | bytes 4976644
  268.3 5.1 copy-start.2
  301.1 5.7 copy-start.10
  301.1 208.3 %all-to-all-start.1 = ((bf16[32,96,2304]{2,1,0:T(8,128)(2,1)}), bf16[32,96,2304]{2,1,0:T(8,128)(2,1)}, u32[]{:S(2)}, u32[]{:S(2)}) async-start(bf16[32,96,2304]{2,1,0:T(8,128)(2,1)} %bitcast.79), calls=%async_computation.1 | async-start | bytes 28311552 | tf_op jit(solution)/shard_map/all_to_all | solution.py:142
  306.3 320.4 %reduce-scatter.2.cloned.1.call-start = ((), (), s32[]{:S(2)}) async-start(), calls=%async_computation.4 | async-start | bytes 1474560 | tf_op jit(solution)/shard_map/reduce_scatter | solution.py:152
  556.9 71.7 %copy-start.1 = (bf16[576,2304]{1,0:T(8,128)(2,1)S(1)}, bf16[576,2304]{1,0:T(8,128)(2,1)}, u32[]{:S(2)}) copy-start(bf16[576,2304]{1,0:T(8,128)(2,1)} %param.19) | copy-start | bytes 7962628
Sparse Core Ops, SparseCore 0:
  49.0 50.1 all-reduce.1
  558.4 68.2 reduce-scatter.1
where the time goes:
time: 636 us; the launch traced here: 635 us
  waiting for transfers between devices  314 us (49%)
  blocking collectives  163 us (26%)
  matrix products  57.5 us (9%)
  local copies, waits for them, and re-layouts  51.2 us (8%)
  other arithmetic  29.4 us (5%)
  between operations  14.5 us (2%)
    all_to_all x1, waiting for transfers between devices, per_device(): lax.all_to_all(partial_value.reshape(received.shape), 'req', split_axis=0...  198 us
    all_to_all x1, blocking collectives, per_device(): lax.all_to_all(outgoing, 'req', split_axis=0, concat_axis=0, tiled=True)  163 us
    reduce_scatter x1, waiting for transfers between devices, per_device(): lax.psum_scatter(local_sum.astype(jnp.bfloat16), 'tp', scatter_dimension=...  68.4 us
    psum x1, waiting for transfers between devices, per_device(): lax.psum(jnp.dot(attended, w_out, preferred_element_type=jnp.float32).ast...  47.8 us
    gather x1, local copies, waits for them, and re-layouts, per_device(): fetched = jnp.take(back_rows, back_index, axis=0)  25.2 us
    dot_general x1, matrix products, per_device(): jnp.dot(activation, expert_down[0], preferred_element_type=jnp.float32)  20.6 us
  transfers between devices with their start and end apart: 3, of which 3 were waited for; matrix products, arithmetic and copies ran while one was open for 1% of the time, Pallas kernels for 0%

commit v1 on v0

--- a/solution.py
+++ b/solution.py
@@ -118,37 +118,46 @@
         jnp.int32
     )
     slot_rank = jnp.sum((jnp.cumsum(onehot, axis=0) - onehot) * onehot, axis=1)
-    slot_ids = flat_routes * CAP + slot_rank
+    tp_size = lax.axis_size("tp")
+    core = lax.axis_index("tp") % 2
+    half_cap = CAP // 2
+    pairs = [(i, i ^ 1) for i in range(tp_size)]
+    gate_w = jnp.concatenate([expert_gate[0], lax.ppermute(expert_gate[0], "tp", pairs)], axis=1)
+    up_w = jnp.concatenate([expert_up[0], lax.ppermute(expert_up[0], "tp", pairs)], axis=1)
+    down_w = jnp.concatenate([expert_down[0], lax.ppermute(expert_down[0], "tp", pairs)], axis=0)
+    local_rank = slot_rank - core * half_cap
+    in_half = (local_rank >= 0) & (local_rank < half_cap)
+    slot_ids = jnp.where(in_half, flat_routes * half_cap + local_rank, -1)
     paired = slot_ids.reshape(token_count, TOP)
-    placing = jnp.any(
-        paired[None, :, :] == jnp.arange(expert_count * CAP, dtype=jnp.int32)[:, None, None], axis=2
-    ).astype(jnp.bfloat16)
+    slot_range = jnp.arange(expert_count * half_cap, dtype=jnp.int32)
+    placing = jnp.any(paired[None, :, :] == slot_range[:, None, None], axis=2).astype(jnp.bfloat16)
     packed = (
         jnp.dot(placing, moe_input, preferred_element_type=jnp.float32)
         .astype(jnp.bfloat16)
-        .reshape(expert_count, CAP, model_width)
+        .reshape(expert_count, half_cap, model_width)
     )
-    outgoing = jnp.broadcast_to(packed[:, None], (expert_count, copies, CAP, model_width)).reshape(
-        expert_count * copies, CAP, model_width
+    outgoing = jnp.broadcast_to(packed[:, None], (expert_count, copies, half_cap, model_width)).reshape(
+        expert_count * copies, half_cap, model_width
     )
     received = lax.all_to_all(outgoing, "req", split_axis=0, concat_axis=0, tiled=True)
     token_rows = received.reshape(-1, model_width)
-    gate_proj = jnp.dot(token_rows, expert_gate[0], preferred_element_type=jnp.float32)
-    up_proj = jnp.dot(token_rows, expert_up[0], preferred_element_type=jnp.float32)
+    gate_proj = jnp.dot(token_rows, gate_w, preferred_element_type=jnp.float32)
+    up_proj = jnp.dot(token_rows, up_w, preferred_element_type=jnp.float32)
     activation = (jax.nn.silu(gate_proj) * up_proj).astype(jnp.bfloat16)
-    partial_value = jnp.dot(activation, expert_down[0], preferred_element_type=jnp.float32).astype(
+    partial_value = jnp.dot(activation, down_w, preferred_element_type=jnp.float32).astype(
         jnp.bfloat16
     )
     returned = lax.all_to_all(
         partial_value.reshape(received.shape), "req", split_axis=0, concat_axis=0, tiled=True
     )
-    back_rows = returned.reshape(-1, model_width)
-    back_index = (
-        flat_routes[None, :] * copies + jnp.arange(copies, dtype=jnp.int32)[:, None]
-    ) * CAP + slot_rank[None, :]
-    fetched = jnp.take(back_rows, back_index, axis=0)
-    summed = jnp.sum(fetched.astype(jnp.float32), axis=0).reshape(token_count, TOP, model_width)
-    local_sum = first_gate[:, None] * summed[:, 0] + second_gate[:, None] * summed[:, 1]
+    summed = jnp.sum(
+        returned.reshape(expert_count, copies, half_cap, model_width).astype(jnp.float32), axis=1
+    ).reshape(expert_count * half_cap, model_width)
+    gates = jnp.stack([first_gate, second_gate], axis=1)
+    mixing = jnp.sum(
+        jnp.where(paired[:, :, None] == slot_range[None, None, :], gates[:, :, None], 0.0), axis=1
+    )
+    local_sum = jnp.dot(mixing, summed, precision=lax.Precision.HIGHEST)
     moe_own = lax.psum_scatter(
         local_sum.astype(jnp.bfloat16), "tp", scatter_dimension=0, tiled=True
     ).astype(jnp.float32)

time: 636 us -> 402 us (0.63)
  blocking collectives: 163 us -> 0 us
  local copies, waits for them, and re-layouts: 51.2 us -> 8.63 us
  waiting for transfers between devices: 314 us -> 272 us
  starting transfers between devices: 5.26 us -> 16.9 us
  matrix products: 57.5 us -> 65.5 us
    all_to_all x1 -> x0, blocking collectives: 163 us -> none  [per_device(): lax.all_to_all(outgoing, 'req', split_axis=0, concat_axis=0, tiled=True)]
    all_to_all x1, waiting for transfers between devices: 198 us -> 87.7 us  [per_device(): lax.all_to_all(partial_value.reshape(received.shape), 'req', split_axis=0...]
    all_to_all x0 -> x1, waiting for transfers between devices: none -> 97.1 us  [per_device(): lax.all_to_all(outgoing, 'req', split_axis=0, concat_axis=0, tiled=True)]
    reduce_scatter x1, waiting for transfers between devices: 68.4 us -> 35.9 us  [per_device(): lax.psum_scatter(local_sum.astype(jnp.bfloat16), 'tp', scatter_dimension=...]
    gather x1 -> x0, local copies, waits for them, and re-layouts: 25.2 us -> none  [per_device(): fetched = jnp.take(back_rows, back_index, axis=0)]
    dot_general x2 -> x3, matrix products: 27.6 us -> 36.1 us  [the longest x1 21.1 us: per_device(): jnp.dot(activation, down_w, preferred_element_type=jnp.float32)]
    slice x2 -> x1, local copies, waits for them, and re-layouts: 8.03 us -> 0.21 us  [the longest x1 7.82 us: per_device(): summed[:, 0]]
    all_to_all x0 -> x1, starting transfers between devices: none -> 7.02 us  [per_device(): lax.all_to_all(outgoing, 'req', split_axis=0, concat_axis=0, tiled=True)]
  transfers between devices with their start and end apart: 3 -> 7, of which waited for: 3 -> 5; matrix products, arithmetic and copies ran while one was open for 1% -> 4% of each run, Pallas kernels for 0% -> 0%
where the time goes in v1:
time: 402 us
  waiting for transfers between devices  272 us (68%)
  matrix products  65.5 us (16%)
  other arithmetic  24.3 us (6%)
  starting transfers between devices  16.9 us (4%)
  between operations  14.5 us (4%)
  local copies, waits for them, and re-layouts  8.63 us (2%)
    all_to_all x1, waiting for transfers between devices, per_device(): lax.all_to_all(outgoing, 'req', split_axis=0, concat_axis=0, tiled=True)  97.1 us
    all_to_all x1, waiting for transfers between devices, per_device(): lax.all_to_all(partial_value.reshape(received.shape), 'req', split_axis=0...  87.7 us
    psum x1, waiting for transfers between devices, per_device(): lax.psum(jnp.dot(attended, w_out, preferred_element_type=jnp.float32).ast...  48 us
    reduce_scatter x1, waiting for transfers between devices, per_device(): lax.psum_scatter(local_sum.astype(jnp.bfloat16), 'tp', scatter_dimension=...  35.9 us
    dot_general x1, matrix products, per_device(): jnp.dot(activation, down_w, preferred_element_type=jnp.float32)  21.1 us
    reduce_sum x1, other arithmetic, attention(): totals = jnp.sum(weights, axis=-1)  10.6 us
    dot_general x1, matrix products, attention(): jnp.einsum('hqk,khd->qhd', weights.astype(jnp.bfloat16), all_values, pref...  10 us
    dot_general x1, matrix products, per_device(): gate_proj = jnp.dot(token_rows, gate_w, preferred_element_type=jnp.float32)  9.94 us
  transfers between devices with their start and end apart: 7, of which 5 were waited for; matrix products, arithmetic and copies ran while one was open for 4% of the time, Pallas kernels for 0%

profile of v1, /device:TPU:1, one launch (start us, length us, event | category | flops | bytes accessed | tf_op | source)
XLA Modules:
  0.0 401.6 jit_solution(16575954713709232016)
XLA Ops:
  6.5 0.0 copy-start
  6.5 0.0 all-reduce.2.cloned.1.call-start
  6.6 1.7 fusion.28
  8.3 6.0 %convolution_bitcast_fusion = f32[3,256,576]{1,2,0:T(8,128)S(1)} fusion(bf16[3,2304,576]{1,2,0:T(8,128)(2,1)} %param.18, bf16[256,2304]{1,0:T(8,128)(2,1)} %param.13, f32[2304]{0:T(1024)} %param.17, f32[256]{0:T(256)S(1)} %add_rsqrt_fusion.1), kind=kOutput, calls=%fused_computation.44 | convolution fusion | flops 2040791040 | bytes 10921984 | tf_op jit(solution)/shard_map/td,cdh->cth/dot_general | solution.py:89
  14.3 0.0 copy-start.5
  14.3 0.1 fusion.69
  15.3 0.2 multiply_cosine_fusion
  15.5 0.4 fusion.31
  15.9 0.2 subtract_convert_fusion.1
  16.1 0.0 copy-done.5
  16.1 9.9 %fusion = (f32[9,256]{1,0:T(8,128)S(1)}, f32[9,256,2304]{2,1,0:T(8,128)}) fusion(pred[256,2304]{1,0:T(8,128)(4,1)S(1)} %fusion.31, bf16[256,9,32]{0,2,1:T(8,128)(2,1)S(1)} %get-tuple-element.13, bf16[256,9,32]{0,2,1:T(8,128)(2,1)S(1)} %get-tuple-element.14, bf16[2048,9,64]{0,2,1:T(8,128)(2,1)S(1)} %bitcast.62, ...), kind=kOutput, calls=%fused_computation.3 | convolution fusion | flops 703952640 | bytes 24781824 | tf_op jit(solution)/shard_map/qhd,khd->hqk/dot_general | solution.py:43
  26.0 10.6 %fusion.1 = f32[9,256]{1,0:T(8,128)S(1)} fusion(f32[9,256,2304]{2,1,0:T(8,128)} %get-tuple-element.20, f32[9,256]{1,0:T(8,128)S(1)} %get-tuple-element.19, pred[256,2304]{1,0:T(8,128)(4,1)S(1)} %fusion.31), kind=kLoop, calls=%fused_computation.4 | loop fusion | flops 21231360 | bytes 21841920 | tf_op jit(solution)/shard_map/reduce_sum | solution.py:56
  36.6 0.0 copy-done.6
  36.6 10.0 %fusion.48 = bf16[256,9,64]{0,2,1:T(8,128)(2,1)S(1)} fusion(f32[9,256,2304]{2,1,0:T(8,128)} %get-tuple-element.20, f32[9,256]{1,0:T(8,128)S(1)} %get-tuple-element.19, pred[256,2304]{1,0:T(8,128)(4,1)S(1)} %fusion.31, bf16[256,9,64]{0,2,1:T(8,128)(2,1)S(1)} %bitcast.60, bf16[2048,9,64]{0,2,1:T(8,128)(2,1)S(1)} %bitcast.63, f32[256,9]{0,1:T(8,128)S(1)} %bitcast.61), kind=kOutput, calls=%fused_computation.50 | convolution fusion | flops 706314240 | bytes 24791040 | tf_op jit(solution)/shard_map/hqk,khd->qhd/dot_general | solution.py:57
  46.6 0.0 copy-done
  46.7 0.0 copy-start.4
  46.7 2.2 convolution_convert_fusion.3
  48.8 0.0 all-reduce.2.cloned.1.call-update
  48.9 0.0 copy-done.4
  48.9 0.1 copy.50
  49.0 0.1 eq.57
  49.2 0.0 copy-start.8
  49.2 0.1 eq.53
  49.3 1.1 reduce-window.6
  50.5 0.2 slice_reduce_fusion
  50.7 0.1 fusion.58
  50.9 0.1 sub.49
  51.0 0.1 copy.52
  51.1 0.1 fusion.53
  51.2 48.0 %all-reduce.2.cloned.1.call-done = bf16[256,2304]{1,0:T(8,128)(2,1)} async-done(((bf16[256,2304]{1,0:T(8,128)(2,1)}), bf16[256,2304]{1,0:T(8,128)(2,1)}) %all-reduce.2.cloned.1.call-update) | async-done | bytes 1179664 | tf_op jit(solution)/shard_map/psum | solution.py:106
  99.3 0.0 copy-done.2
  99.3 3.1 convert_add_fusion
  102.4 0.0 copy-done.8
  102.4 0.0 copy-done.3
  102.4 0.8 convolution_convert_fusion.1
  103.2 3.5 broadcast_in_dim.87
  106.7 7.0 %all-to-all-start = ((bf16[32,48,2304]{2,1,0:T(8,128)(2,1)}), bf16[32,48,2304]{2,1,0:T(8,128)(2,1)}, u32[]{:S(2)}, u32[]{:S(2)}) async-start(bf16[32,48,2304]{2,1,0:T(8,128)(2,1)} %bitcast.53), calls=%async_computation | async-start | bytes 14155776 | tf_op jit(solution)/shard_map/all_to_all | solution.py:142
  113.7 0.5 collective-permute-start
  114.2 0.1 collective-permute-start.2
  114.3 0.4 collective-permute-start.1
  114.7 3.0 collective-permute-done
  117.7 97.1 %all-to-all-done = bf16[32,48,2304]{2,1,0:T(8,128)(2,1)} async-done(((bf16[32,48,2304]{2,1,0:T(8,128)(2,1)}), bf16[32,48,2304]{2,1,0:T(8,128)(2,1)}, u32[]{:S(2)}, u32[]{:S(2)}) %all-to-all-start) | async-done | bytes 7077920 | tf_op jit(solution)/shard_map/all_to_all | solution.py:142
  214.9 9.9 %fusion.6 = f32[1536,720]{0,1:T(8,128)} fusion(bf16[1536,2304]{1,0:T(8,128)(2,1)} %bitcast.16, bf16[2304,360]{0,1:T(8,128)(2,1)} %collective-permute-done, bf16[2304,360]{0,1:T(8,128)(2,1)} %bitcast.65), kind=kOutput, calls=%fused_computation.17 | convolution fusion | flops 5102714880 | bytes 14819328 | tf_op jit(solution)/shard_map/dot_general | solution.py:144
  224.8 0.0 collective-permute-done.2
  224.8 0.0 collective-permute-done.1
  224.8 21.1 %convolution_convert_fusion = bf16[1536,2304]{1,0:T(8,128)(2,1)} fusion(bf16[360,2304]{1,0:T(8,128)(2,1)} %collective-permute-done.2, bf16[360,2304]{1,0:T(8,128)(2,1)} %bitcast.67, f32[1536,720]{0,1:T(8,128)} %fusion.6, bf16[1536,2304]{1,0:T(8,128)(2,1)} %bitcast.16, bf16[2304,360]{0,1:T(8,128)(2,1)} %collective-permute-done.1, bf16[2304,360]{0,1:T(8,128)(2,1)} %bitcast.69), kind=kOutput, calls=%fused_computation.7 | convolution fusion | flops 10215604224 | bytes 25214976 | tf_op jit(solution)/shard_map/dot_general | solution.py:147
  245.9 8.8 %all-to-all-start.1 = ((bf16[32,48,2304]{2,1,0:T(8,128)(2,1)}), bf16[32,48,2304]{2,1,0:T(8,128)(2,1)}, u32[]{:S(2)}, u32[]{:S(2)}) async-start(bf16[32,48,2304]{2,1,0:T(8,128)(2,1)} %bitcast.55), calls=%async_computation.1 | async-start | bytes 14155776 | tf_op jit(solution)/shard_map/all_to_all | solution.py:150
  254.7 0.0 reduce-scatter.2.cloned.1.call-start
  254.8 0.1 copy.55
  254.9 0.1 reshape.221
  255.1 0.0 copy-done.7
  255.1 0.5 fusion.68
  255.6 3.7 gather_fusion
  259.3 0.1 reshape.224
  259.5 0.1 copy.56
  259.6 0.2 select_reduce_fusion
  259.8 87.7 %all-to-all-done.1 = bf16[32,48,2304]{2,1,0:T(8,128)(2,1)} async-done(((bf16[32,48,2304]{2,1,0:T(8,128)(2,1)}), bf16[32,48,2304]{2,1,0:T(8,128)(2,1)}, u32[]{:S(2)}, u32[]{:S(2)}) %all-to-all-start.1) | async-done | bytes 7077920 | tf_op jit(solution)/shard_map/all_to_all | solution.py:150
  347.5 4.4 %convert_reduce_fusion = f32[8,48,2304]{2,1,0:T(8,128)S(1)} fusion(bf16[32,48,2304]{2,1,0:T(8,128)(2,1)} %all-to-all-done.1), kind=kLoop, calls=%fused_computation.6 | loop fusion | flops 6193152 | bytes 10616832 | tf_op jit(solution)/shard_map/reduce_sum | solution.py:153
  351.9 0.0 copy-start.1
  351.9 5.0 %convolution_convert_fusion.2 = bf16[256,2304]{1,0:T(8,128)(2,1)} fusion(f32[256,384]{1,0:T(8,128)S(1)} %select_reduce_fusion, f32[384,2304]{1,0:T(8,128)S(1)} %bitcast.54), kind=kOutput, calls=%fused_computation.12 | convolution fusion | flops 2718498816 | bytes 5111808 | tf_op jit(solution)/shard_map/dot_general | solution.py:160
  356.9 0.0 reduce-scatter.2.cloned.1.call-update
  357.0 35.9 %reduce-scatter.2.cloned.1.call-done = bf16[64,2304]{1,0:T(8,128)(2,1)} async-done(((bf16[256,2304]{1,0:T(8,128)(2,1)}), bf16[64,2304]{1,0:T(8,128)(2,1)}) %reduce-scatter.2.cloned.1.call-update) | async-done | bytes 294928 | tf_op jit(solution)/shard_map/reduce_scatter | solution.py:161
  392.9 1.9 add_convert_fusion
  394.8 0.0 copy-done.1
  (20 shorter events, 0.2 us)
Async XLA Ops:
  6.5 40.1 %copy-start = (bf16[576,2304]{1,0:T(8,128)(2,1)S(1)}, bf16[576,2304]{1,0:T(8,128)(2,1)}, u32[]{:S(2)}) copy-start(bf16[576,2304]{1,0:T(8,128)(2,1)} %param.19) | copy-start | bytes 7962628
  6.5 92.7 %all-reduce.2.cloned.1.call-start = ((), (), s32[]{:S(2)}) async-start(), calls=%async_computation.3 | async-start | bytes 2359296 | tf_op jit(solution)/shard_map/psum | solution.py:106
  14.3 1.7 copy-start.5
  26.0 10.6 %copy-start.6 = (bf16[1,2048,576]{1,2,0:T(8,128)(2,1)S(1)}, bf16[1,2048,576]{1,2,0:T(8,128)(2,1)}, u32[]{:S(2)}) copy-start(bf16[1,2048,576]{1,2,0:T(8,128)(2,1)} %param.16) | copy-start | bytes 7077892
  46.7 2.2 copy-start.4
  48.8 50.4 %copy-start.2 = (bf16[256,2304]{1,0:T(8,128)(2,1)S(1)}, bf16[256,2304]{1,0:T(8,128)(2,1)}, u32[]{:S(2)}) copy-start(bf16[256,2304]{1,0:T(8,128)(2,1)} %param.13) | copy-start | bytes 3538948
  49.2 53.2 %copy-start.8 = (f32[2304]{0:T(1024)S(1)}, f32[2304]{0:T(1024)}, u32[]{:S(2)}) copy-start(f32[2304]{0:T(1024)} %param.20) | copy-start | bytes 27652
  99.3 3.1 copy-start.3
  106.7 108.2 %all-to-all-start = ((bf16[32,48,2304]{2,1,0:T(8,128)(2,1)}), bf16[32,48,2304]{2,1,0:T(8,128)(2,1)}, u32[]{:S(2)}, u32[]{:S(2)}) async-start(bf16[32,48,2304]{2,1,0:T(8,128)(2,1)} %bitcast.53), calls=%async_computation | async-start | bytes 14155776 | tf_op jit(solution)/shard_map/all_to_all | solution.py:142
  113.7 4.0 %collective-permute-start = (bf16[2304,360]{0,1:T(8,128)(2,1)}, bf16[2304,360]{0,1:T(8,128)(2,1)}, u32[]{:S(2)}, u32[]{:S(2)}) collective-permute-start(bf16[2304,360]{0,1:T(8,128)(2,1)} %bitcast.64), channel_id=1, source_target_pairs={{0,1},{1,0},{2,3},{3,2},{4,5},{5,4},{6,7},{7,6},{8,9},{9,8},{10,11... | collective-permute-start | bytes 4976648 | tf_op jit(solution)/shard_map/ppermute | solution.py:125
  114.2 110.6 %collective-permute-start.2 = (bf16[360,2304]{1,0:T(8,128)(2,1)}, bf16[360,2304]{1,0:T(8,128)(2,1)}, u32[]{:S(2)}, u32[]{:S(2)}) collective-permute-start(bf16[360,2304]{1,0:T(8,128)(2,1)} %bitcast.66), channel_id=1, source_target_pairs={{0,1},{1,0},{2,3},{3,2},{4,5},{5,4},{6,7},{7,6},{8,9},{9,8},{10,11... | collective-permute-start | bytes 4976648 | tf_op jit(solution)/shard_map/ppermute | solution.py:127
  114.3 110.5 %collective-permute-start.1 = (bf16[2304,360]{0,1:T(8,128)(2,1)}, bf16[2304,360]{0,1:T(8,128)(2,1)}, u32[]{:S(2)}, u32[]{:S(2)}) collective-permute-start(bf16[2304,360]{0,1:T(8,128)(2,1)} %bitcast.68), channel_id=1, source_target_pairs={{0,1},{1,0},{2,3},{3,2},{4,5},{5,4},{6,7},{7,6},{8,9},{9,8},{10,11... | collective-permute-start | bytes 4976648 | tf_op jit(solution)/shard_map/ppermute | solution.py:126
  245.9 9.1 %copy-start.7 = (bf16[2304,8]{0,1:T(8,128)(2,1)S(1)}, bf16[2304,8]{0,1:T(8,128)(2,1)}, u32[]{:S(2)}) copy-start(bf16[2304,8]{0,1:T(8,128)(2,1)} %param.21) | copy-start | bytes 110596
  245.9 101.6 %all-to-all-start.1 = ((bf16[32,48,2304]{2,1,0:T(8,128)(2,1)}), bf16[32,48,2304]{2,1,0:T(8,128)(2,1)}, u32[]{:S(2)}, u32[]{:S(2)}) async-start(bf16[32,48,2304]{2,1,0:T(8,128)(2,1)} %bitcast.55), calls=%async_computation.1 | async-start | bytes 14155776 | tf_op jit(solution)/shard_map/all_to_all | solution.py:150
  254.7 138.1 %reduce-scatter.2.cloned.1.call-start = ((), (), s32[]{:S(2)}) async-start(), calls=%async_computation.4 | async-start | bytes 1474560 | tf_op jit(solution)/shard_map/reduce_scatter | solution.py:161
  351.9 42.8 %copy-start.1 = (bf16[576,2304]{1,0:T(8,128)(2,1)S(1)}, bf16[576,2304]{1,0:T(8,128)(2,1)}, u32[]{:S(2)}) copy-start(bf16[576,2304]{1,0:T(8,128)(2,1)} %param.19) | copy-start | bytes 7962628
Sparse Core Ops, SparseCore 0:
  49.0 50.2 all-reduce.1
  357.1 35.7 reduce-scatter.1

commit v2 on v1

--- a/solution.py
+++ b/solution.py
@@ -58,6 +58,42 @@
         "hqk,khd->qhd", weights.astype(jnp.bfloat16), all_values, preferred_element_type=jnp.float32
     )
     return (mixture / jnp.transpose(totals)[:, :, None]).astype(jnp.bfloat16)
+
+
+def tp_allreduce(partial):
+    tp_size = lax.axis_size("tp")
+    core = lax.axis_index("tp") % 2
+    core_pairs = [(i, i ^ 1) for i in range(tp_size)]
+    z_pairs = [(i, i ^ 2) for i in range(tp_size)]
+    halves = partial.astype(jnp.bfloat16).reshape(2, partial.shape[0] // 2, partial.shape[1])
+    keep = jnp.where(core == 0, halves[0], halves[1])
+    send = jnp.where(core == 0, halves[1], halves[0])
+    chip_sum = (
+        keep.astype(jnp.float32) + lax.ppermute(send, "tp", core_pairs).astype(jnp.float32)
+    ).astype(jnp.bfloat16)
+    total = (
+        chip_sum.astype(jnp.float32) + lax.ppermute(chip_sum, "tp", z_pairs).astype(jnp.float32)
+    ).astype(jnp.bfloat16)
+    other = lax.ppermute(total, "tp", core_pairs)
+    return jnp.where(core == 0, jnp.concatenate([total, other]), jnp.concatenate([other, total]))
+
+
+def tp_reduce_scatter(partial):
+    tp_size = lax.axis_size("tp")
+    tp_index = lax.axis_index("tp")
+    core = tp_index % 2
+    upper = tp_index // 2
+    core_pairs = [(i, i ^ 1) for i in range(tp_size)]
+    z_pairs = [(i, i ^ 2) for i in range(tp_size)]
+    blocks = partial.astype(jnp.bfloat16).reshape(2, 2, partial.shape[0] // 4, partial.shape[1])
+    keep = jnp.where(core == 0, blocks[:, 0], blocks[:, 1])
+    send = jnp.where(core == 0, blocks[:, 1], blocks[:, 0])
+    chip_sum = (
+        keep.astype(jnp.float32) + lax.ppermute(send, "tp", core_pairs).astype(jnp.float32)
+    ).astype(jnp.bfloat16)
+    mine = jnp.where(upper == 0, chip_sum[0], chip_sum[1])
+    theirs = jnp.where(upper == 0, chip_sum[1], chip_sum[0])
+    return mine.astype(jnp.float32) + lax.ppermute(theirs, "tp", z_pairs).astype(jnp.float32)
 
 
 def per_device(
@@ -103,8 +139,8 @@
         [value_cache[0].reshape(cache_len, local_heads, HEAD), fresh_values], axis=0
     )
     attended = attention(queries, all_keys, all_values, length).reshape(token_count, local_lanes)
-    summed_attn = lax.psum(
-        jnp.dot(attended, w_out, preferred_element_type=jnp.float32).astype(jnp.bfloat16), "tp"
+    summed_attn = tp_allreduce(
+        jnp.dot(attended, w_out, preferred_element_type=jnp.float32)
     ).astype(jnp.float32)
     updated = residual + summed_attn
     moe_input = normalize(updated, ffn_norm).astype(jnp.bfloat16)
@@ -158,9 +194,7 @@
         jnp.where(paired[:, :, None] == slot_range[None, None, :], gates[:, :, None], 0.0), axis=1
     )
     local_sum = jnp.dot(mixing, summed, precision=lax.Precision.HIGHEST)
-    moe_own = lax.psum_scatter(
-        local_sum.astype(jnp.bfloat16), "tp", scatter_dimension=0, tiled=True
-    ).astype(jnp.float32)
+    moe_own = tp_reduce_scatter(local_sum)
     return (own_residual + moe_own).astype(jnp.bfloat16)
 
 

time: 402 us -> 347 us (0.86)
  waiting for transfers between devices: 272 us -> 210 us
  starting transfers between devices: 16.9 us -> 31 us
  between operations: 14.5 us -> 0.95 us
  other arithmetic: 24.3 us -> 29.9 us
    psum x1 -> x0, waiting for transfers between devices: 48 us -> none  [per_device(): lax.psum(jnp.dot(attended, w_out, preferred_element_type=jnp.float32).ast...]
    reduce_scatter x1 -> x0, waiting for transfers between devices: 35.9 us -> none  [per_device(): lax.psum_scatter(local_sum.astype(jnp.bfloat16), 'tp', scatter_dimension=...]
    ppermute x0 -> x5, waiting for transfers between devices: none -> 23.4 us  [the longest x1 11.6 us: tp_allreduce(): lax.ppermute(chip_sum, 'tp', z_pairs).astype(jnp.float32)]
    ppermute x0 -> x5, starting transfers between devices: none -> 12.4 us  [the longest x1 3.76 us: tp_allreduce(): lax.ppermute(chip_sum, 'tp', z_pairs).astype(jnp.float32)]
  transfers between devices with their start and end apart: 7 -> 10, of which waited for: 5 -> 8; matrix products, arithmetic and copies ran while one was open for 4% -> 5% of each run, Pallas kernels for 0% -> 0%
where the time goes in v2:
time: 347 us
  waiting for transfers between devices  210 us (61%)
  matrix products  64.2 us (19%)
  starting transfers between devices  31 us (9%)
  other arithmetic  29.9 us (9%)
  local copies, waits for them, and re-layouts  10.3 us (3%)
    all_to_all x1, waiting for transfers between devices, per_device(): lax.all_to_all(outgoing, 'req', split_axis=0, concat_axis=0, tiled=True)  95.6 us
    all_to_all x1, waiting for transfers between devices, per_device(): lax.all_to_all(partial_value.reshape(received.shape), 'req', split_axis=0...  88.3 us
    dot_general x1, matrix products, per_device(): jnp.dot(activation, down_w, preferred_element_type=jnp.float32)  21.1 us
    ppermute x1, waiting for transfers between devices, tp_allreduce(): lax.ppermute(chip_sum, 'tp', z_pairs).astype(jnp.float32)  11.6 us
    dot_general x1, matrix products, attention(): jnp.einsum('qhd,khd->hqk', queries, all_keys, preferred_element_type=jnp....  10.8 us
    reduce_sum x1, other arithmetic, attention(): totals = jnp.sum(weights, axis=-1)  10.6 us
    dot_general x1, matrix products, attention(): jnp.einsum('hqk,khd->qhd', weights.astype(jnp.bfloat16), all_values, pref...  10 us
    dot_general x1, matrix products, per_device(): gate_proj = jnp.dot(token_rows, gate_w, preferred_element_type=jnp.float32)  9.94 us
  transfers between devices with their start and end apart: 10, of which 8 were waited for; matrix products, arithmetic and copies ran while one was open for 5% of the time, Pallas kernels for 0%

profile of v2, /device:TPU:1, one launch (start us, length us, event | category | flops | bytes accessed | tf_op | source)
XLA Modules:
  0.0 346.6 jit_solution(17172669155078594993)
XLA Ops:
  0.0 0.6 multiply_exponential_fusion
  0.6 1.8 fusion.28
  2.4 6.0 %convolution_bitcast_fusion = f32[3,256,576]{1,2,0:T(8,128)S(1)} fusion(bf16[3,2304,576]{1,2,0:T(8,128)(2,1)} %param.18, bf16[256,2304]{1,0:T(8,128)(2,1)} %param.13, f32[2304]{0:T(1024)} %param.17, f32[256]{0:T(256)S(1)} %add_rsqrt_fusion.1), kind=kOutput, calls=%fused_computation.44 | convolution fusion | flops 2040791040 | bytes 10921984 | tf_op jit(solution)/shard_map/td,cdh->cth/dot_general | solution.py:125
  8.4 0.9 fusion.72
  10.0 0.6 add_convert_fusion.4
  10.6 0.6 iota_compare_fusion.5
  11.1 0.9 multiply_cosine_fusion
  12.0 1.1 fusion.31
  13.1 1.2 subtract_convert_fusion.1
  14.3 10.8 %fusion = (f32[9,256]{1,0:T(8,128)S(1)}, f32[9,256,2304]{2,1,0:T(8,128)}) fusion(pred[256,2304]{1,0:T(8,128)(4,1)S(1)} %fusion.31, bf16[256,9,32]{0,2,1:T(8,128)(2,1)S(1)} %get-tuple-element.13, bf16[256,9,32]{0,2,1:T(8,128)(2,1)S(1)} %get-tuple-element.14, bf16[2048,9,64]{0,2,1:T(8,128)(2,1)} %bitcast.87, bf16[256,9,32]{0,2,1:T(8,128)(2,1)S(1)} %get-tuple-element.10, ...), kind=kOutput, calls=%fused_computation.3 | convolution fusion | flops 703952640 | bytes 24781824 | tf_op jit(solution)/shard_map/qhd,khd->hqk/dot_general | solution.py:43
  25.2 10.6 %fusion.1 = f32[9,256]{1,0:T(8,128)S(1)} fusion(f32[9,256,2304]{2,1,0:T(8,128)} %get-tuple-element.20, f32[9,256]{1,0:T(8,128)S(1)} %get-tuple-element.19, pred[256,2304]{1,0:T(8,128)(4,1)S(1)} %fusion.31), kind=kLoop, calls=%fused_computation.4 | loop fusion | flops 21231360 | bytes 21841920 | tf_op jit(solution)/shard_map/reduce_sum | solution.py:56
  35.8 10.0 %fusion.49 = bf16[256,9,64]{0,2,1:T(8,128)(2,1)S(1)} fusion(f32[9,256,2304]{2,1,0:T(8,128)} %get-tuple-element.20, f32[9,256]{1,0:T(8,128)S(1)} %get-tuple-element.19, pred[256,2304]{1,0:T(8,128)(4,1)S(1)} %fusion.31, bf16[256,9,64]{0,2,1:T(8,128)(2,1)S(1)} %bitcast.85, bf16[2048,9,64]{0,2,1:T(8,128)(2,1)S(1)} %bitcast.88, f32[256,9]{0,1:T(8,128)S(1)} %bitcast.86), kind=kOutput, calls=%fused_computation.55 | convolution fusion | flops 706314240 | bytes 24791040 | tf_op jit(solution)/shard_map/hqk,khd->qhd/dot_general | solution.py:57
  45.8 1.1 convolution_convert_fusion.3
  47.0 0.0 copy-start.6
  47.0 0.1 broadcast_select_fusion
  47.0 1.5 collective-permute-start
  48.5 1.6 collective-permute-done
  50.2 0.3 add_convert_fusion.1
  50.4 3.8 %collective-permute-start.1 = (bf16[128,2304]{1,0:T(8,128)(2,1)S(1)}, bf16[128,2304]{1,0:T(8,128)(2,1)S(1)}, u32[]{:S(2)}, u32[]{:S(2)}) collective-permute-start(bf16[128,2304]{1,0:T(8,128)(2,1)S(1)} %add_convert_fusion.1), channel_id=1, source_target_pairs={{0,2},{1,3},{2,0},{3,1},{4,6},{5,7},{6,4},{7,5},{8,10},{9,11},{10,... | collective-permute-start | bytes 1769480 | tf_op jit(solution)/shard_map/ppermute | solution.py:75
  54.2 0.1 copy.56
  54.3 0.1 eq.72
  54.5 0.1 eq.68
  54.6 1.1 reduce-window.6
  55.8 0.2 slice_reduce_fusion
  56.0 11.6 %collective-permute-done.1 = bf16[128,2304]{1,0:T(8,128)(2,1)S(1)} collective-permute-done((bf16[128,2304]{1,0:T(8,128)(2,1)S(1)}, bf16[128,2304]{1,0:T(8,128)(2,1)S(1)}, u32[]{:S(2)}, u32[]{:S(2)}) %collective-permute-start.1) | collective-permute-done | bytes 589856 | tf_op jit(solution)/shard_map/ppermute | solution.py:75
  67.6 0.1 add_convert_fusion
  67.7 0.0 copy-start.4
  67.7 1.1 collective-permute-start.2
  68.9 0.1 fusion.61
  69.0 0.1 sub.54
  69.1 0.1 copy.58
  69.2 0.1 fusion.54
  69.4 1.3 collective-permute-done.2
  70.7 2.2 multiply_reduce_fusion
  72.9 0.7 convolution_convert_fusion.1
  73.6 3.5 broadcast_in_dim.87
  77.1 7.9 %all-to-all-start = ((bf16[32,48,2304]{2,1,0:T(8,128)(2,1)}), bf16[32,48,2304]{2,1,0:T(8,128)(2,1)}, u32[]{:S(2)}, u32[]{:S(2)}) async-start(bf16[32,48,2304]{2,1,0:T(8,128)(2,1)} %bitcast.76), calls=%async_computation | async-start | bytes 14155776 | tf_op jit(solution)/shard_map/all_to_all | solution.py:178
  85.0 0.7 collective-permute-start.3
  85.7 0.1 collective-permute-start.4
  85.8 0.4 collective-permute-start.5
  86.2 3.0 collective-permute-done.3
  89.2 95.6 %all-to-all-done = bf16[32,48,2304]{2,1,0:T(8,128)(2,1)} async-done(((bf16[32,48,2304]{2,1,0:T(8,128)(2,1)}), bf16[32,48,2304]{2,1,0:T(8,128)(2,1)}, u32[]{:S(2)}, u32[]{:S(2)}) %all-to-all-start) | async-done | bytes 7077920 | tf_op jit(solution)/shard_map/all_to_all | solution.py:178
  184.8 9.9 %fusion.6 = f32[1536,720]{0,1:T(8,128)} fusion(bf16[1536,2304]{1,0:T(8,128)(2,1)} %bitcast.16, bf16[2304,360]{0,1:T(8,128)(2,1)} %collective-permute-done.3, bf16[2304,360]{0,1:T(8,128)(2,1)} %bitcast.90), kind=kOutput, calls=%fused_computation.17 | convolution fusion | flops 5102714880 | bytes 14819328 | tf_op jit(solution)/shard_map/dot_general | solution.py:180
  194.7 0.0 collective-permute-done.4
  194.7 21.1 %convolution_convert_fusion = bf16[1536,2304]{1,0:T(8,128)(2,1)} fusion(bf16[360,2304]{1,0:T(8,128)(2,1)} %collective-permute-done.5, bf16[360,2304]{1,0:T(8,128)(2,1)} %bitcast.92, f32[1536,720]{0,1:T(8,128)} %fusion.6, bf16[1536,2304]{1,0:T(8,128)(2,1)} %bitcast.16, bf16[2304,360]{0,1:T(8,128)(2,1)} %collective-permute-done.4, bf16[2304,360]{0,1:T(8,128)(2,1)} %bitcast.94), kind=kOutput, calls=%fused_computation.7 | convolution fusion | flops 10215604224 | bytes 25214976 | tf_op jit(solution)/shard_map/dot_general | solution.py:183
  215.8 9.5 %all-to-all-start.1 = ((bf16[32,48,2304]{2,1,0:T(8,128)(2,1)}), bf16[32,48,2304]{2,1,0:T(8,128)(2,1)}, u32[]{:S(2)}, u32[]{:S(2)}) async-start(bf16[32,48,2304]{2,1,0:T(8,128)(2,1)} %bitcast.80), calls=%async_computation.1 | async-start | bytes 14155776 | tf_op jit(solution)/shard_map/all_to_all | solution.py:186
  225.4 0.1 copy.61
  225.5 0.1 reshape.244
  225.7 0.5 fusion.71
  226.1 3.5 %gather_fusion = f32[512]{0:T(512)S(1)} fusion(f32[256,8]{0,1:T(8,128)S(1)} %fusion.71, s32[512]{0:T(512)S(1)} %reshape.244), kind=kCustom, calls=%fused_computation | custom fusion | bytes 8192 | tf_op jit(solution)/shard_map/jit(take_along_axis)/gather | solution.py:149
  229.7 0.1 reshape.247
  229.9 0.1 copy.62
  230.0 0.2 select_reduce_fusion
  230.2 88.3 %all-to-all-done.1 = bf16[32,48,2304]{2,1,0:T(8,128)(2,1)} async-done(((bf16[32,48,2304]{2,1,0:T(8,128)(2,1)}), bf16[32,48,2304]{2,1,0:T(8,128)(2,1)}, u32[]{:S(2)}, u32[]{:S(2)}) %all-to-all-start.1) | async-done | bytes 7077920 | tf_op jit(solution)/shard_map/all_to_all | solution.py:186
  318.5 4.4 %convert_reduce_fusion = f32[8,48,2304]{2,1,0:T(8,128)S(1)} fusion(bf16[32,48,2304]{2,1,0:T(8,128)(2,1)} %all-to-all-done.1), kind=kLoop, calls=%fused_computation.6 | loop fusion | flops 6193152 | bytes 10616832 | tf_op jit(solution)/shard_map/reduce_sum | solution.py:189
  322.9 4.0 %convolution_convert_fusion.2 = bf16[256,2304]{1,0:T(8,128)(2,1)S(1)} fusion(f32[256,384]{1,0:T(8,128)S(1)} %select_reduce_fusion, f32[384,2304]{1,0:T(8,128)S(1)} %bitcast.77), kind=kOutput, calls=%fused_computation.12 | convolution fusion | flops 2718498816 | bytes 5111808 | tf_op jit(solution)/shard_map/dot_general | solution.py:196
  326.9 1.0 copy-done.3
  327.9 0.1 select_bitcast_fusion
  328.0 2.6 collective-permute-start.6
  330.5 1.8 collective-permute-done.6
  332.3 1.6 fusion.41
  334.0 3.4 collective-permute-start.7
  337.4 7.2 %collective-permute-done.7 = bf16[64,2304]{1,0:T(8,128)(2,1)} collective-permute-done((bf16[64,2304]{1,0:T(8,128)(2,1)S(1)}, bf16[64,2304]{1,0:T(8,128)(2,1)}, u32[]{:S(2)}, u32[]{:S(2)}) %collective-permute-start.7) | collective-permute-done | bytes 294944 | tf_op jit(solution)/shard_map/ppermute | solution.py:96
  344.6 2.0 fusion.56
  (28 shorter events, 0.2 us)
Async XLA Ops:
  0.0 45.8 %copy-start = (bf16[576,2304]{1,0:T(8,128)(2,1)S(1)}, bf16[576,2304]{1,0:T(8,128)(2,1)}, u32[]{:S(2)}) copy-start(bf16[576,2304]{1,0:T(8,128)(2,1)} %param.19) | copy-start | bytes 7962628
  25.2 10.6 %copy-start.7 = (bf16[1,2048,576]{1,2,0:T(8,128)(2,1)S(1)}, bf16[1,2048,576]{1,2,0:T(8,128)(2,1)}, u32[]{:S(2)}) copy-start(bf16[1,2048,576]{1,2,0:T(8,128)(2,1)} %param.16) | copy-start | bytes 7077892
  47.0 7.2 %copy-start.6 = (s32[256,2]{0,1:T(2,128)S(1)}, s32[256,2]{0,1:T(2,128)}, u32[]{:S(2)}) copy-start(s32[256,2]{0,1:T(2,128)} %param.22) | copy-start | bytes 6148
  47.0 3.1 collective-permute-start
  50.4 17.2 %collective-permute-start.1 = (bf16[128,2304]{1,0:T(8,128)(2,1)S(1)}, bf16[128,2304]{1,0:T(8,128)(2,1)S(1)}, u32[]{:S(2)}, u32[]{:S(2)}) collective-permute-start(bf16[128,2304]{1,0:T(8,128)(2,1)S(1)} %add_convert_fusion.1), channel_id=1, source_target_pairs={{0,2},{1,3},{2,0},{3,1},{4,6},{5,7},{6,4},{7,5},{8,10},{9,11},{10,... | collective-permute-start | bytes 1769480 | tf_op jit(solution)/shard_map/ppermute | solution.py:75
  67.7 5.1 %copy-start.4 = (f32[2304]{0:T(1024)S(1)}, f32[2304]{0:T(1024)}, u32[]{:S(2)}) copy-start(f32[2304]{0:T(1024)} %param.20) | copy-start | bytes 27652
  67.7 2.9 collective-permute-start.2
  72.9 152.8 %copy-start.2 = (f32[256,2304]{1,0:T(8,128)}, f32[256,2304]{1,0:T(8,128)S(1)}, u32[]{:S(2)}) copy-start(f32[256,2304]{1,0:T(8,128)S(1)} %get-tuple-element.6) | copy-start | bytes 7077892
  77.1 107.7 %all-to-all-start = ((bf16[32,48,2304]{2,1,0:T(8,128)(2,1)}), bf16[32,48,2304]{2,1,0:T(8,128)(2,1)}, u32[]{:S(2)}, u32[]{:S(2)}) async-start(bf16[32,48,2304]{2,1,0:T(8,128)(2,1)} %bitcast.76), calls=%async_computation | async-start | bytes 14155776 | tf_op jit(solution)/shard_map/all_to_all | solution.py:178
  85.0 4.2 %collective-permute-start.3 = (bf16[2304,360]{0,1:T(8,128)(2,1)}, bf16[2304,360]{0,1:T(8,128)(2,1)}, u32[]{:S(2)}, u32[]{:S(2)}) collective-permute-start(bf16[2304,360]{0,1:T(8,128)(2,1)} %bitcast.89), channel_id=1, source_target_pairs={{0,1},{1,0},{2,3},{3,2},{4,5},{5,4},{6,7},{7,6},{8,9},{9,8},{10,11... | collective-permute-start | bytes 4976648 | tf_op jit(solution)/shard_map/ppermute | solution.py:161
  85.7 109.0 %collective-permute-start.4 = (bf16[2304,360]{0,1:T(8,128)(2,1)}, bf16[2304,360]{0,1:T(8,128)(2,1)}, u32[]{:S(2)}, u32[]{:S(2)}) collective-permute-start(bf16[2304,360]{0,1:T(8,128)(2,1)} %bitcast.93), channel_id=1, source_target_pairs={{0,1},{1,0},{2,3},{3,2},{4,5},{5,4},{6,7},{7,6},{8,9},{9,8},{10,11... | collective-permute-start | bytes 4976648 | tf_op jit(solution)/shard_map/ppermute | solution.py:162
  85.8 108.9 %collective-permute-start.5 = (bf16[360,2304]{1,0:T(8,128)(2,1)}, bf16[360,2304]{1,0:T(8,128)(2,1)}, u32[]{:S(2)}, u32[]{:S(2)}) collective-permute-start(bf16[360,2304]{1,0:T(8,128)(2,1)} %bitcast.91), channel_id=1, source_target_pairs={{0,1},{1,0},{2,3},{3,2},{4,5},{5,4},{6,7},{7,6},{8,9},{9,8},{10,11... | collective-permute-start | bytes 4976648 | tf_op jit(solution)/shard_map/ppermute | solution.py:163
  215.8 9.8 %copy-start.5 = (bf16[2304,8]{0,1:T(8,128)(2,1)S(1)}, bf16[2304,8]{0,1:T(8,128)(2,1)}, u32[]{:S(2)}) copy-start(bf16[2304,8]{0,1:T(8,128)(2,1)} %param.21) | copy-start | bytes 110596
  215.8 102.6 %all-to-all-start.1 = ((bf16[32,48,2304]{2,1,0:T(8,128)(2,1)}), bf16[32,48,2304]{2,1,0:T(8,128)(2,1)}, u32[]{:S(2)}, u32[]{:S(2)}) async-start(bf16[32,48,2304]{2,1,0:T(8,128)(2,1)} %bitcast.80), calls=%async_computation.1 | async-start | bytes 14155776 | tf_op jit(solution)/shard_map/all_to_all | solution.py:186
  326.9 1.0 copy-start.3
  327.9 18.7 %copy-start.1 = (bf16[576,2304]{1,0:T(8,128)(2,1)S(1)}, bf16[576,2304]{1,0:T(8,128)(2,1)}, u32[]{:S(2)}) copy-start(bf16[576,2304]{1,0:T(8,128)(2,1)} %param.19) | copy-start | bytes 7962628
  328.0 4.3 %collective-permute-start.6 = (bf16[2,64,2304]{2,1,0:T(8,128)(2,1)S(1)}, bf16[2,64,2304]{2,1,0:T(8,128)(2,1)}, u32[]{:S(2)}, u32[]{:S(2)}) collective-permute-start(bf16[2,64,2304]{2,1,0:T(8,128)(2,1)S(1)} %select_bitcast_fusion), channel_id=1, source_target_pairs={{0,1},{1,0},{2,3},{3,2},{4,5},{5,4},{6,7},{7,6},{8,9},{9,8},{10,11... | collective-permute-start | bytes 1769480 | tf_op jit(solution)/shard_map/ppermute | solution.py:92
  334.0 10.6 %collective-permute-start.7 = (bf16[64,2304]{1,0:T(8,128)(2,1)S(1)}, bf16[64,2304]{1,0:T(8,128)(2,1)}, u32[]{:S(2)}, u32[]{:S(2)}) collective-permute-start(bf16[64,2304]{1,0:T(8,128)(2,1)S(1)} %select_bitcast_fusion.1), channel_id=1, source_target_pairs={{0,2},{1,3},{2,0},{3,1},{4,6},{5,7},{6,4},{7,5},{8,10},{9,11},{10,... | collective-permute-start | bytes 884744 | tf_op jit(solution)/shard_map/ppermute | solution.py:96
